TPU v7x, 128 devices: a whole 4x4x4 slice. The times are simulated.
128 devices in a mesh: dap: 4 (over z_lo, core), dp: 32 (over z_hi, y, x).
Axes of the slice: x: 4, y: 4, z: 4 (z_hi: 2, z_lo: 2; z = z_hi * 2 + z_lo), core: 2. Of those that a mesh axis runs over, the one named last changes fastest.
Arguments:
- pair_rep: bfloat16 [32, 128, 128, 128], P('dp', 'dap'), may hold values from -6 to 6
- cotangent: bfloat16 [32, 128, 128, 128], P('dp', 'dap'), may hold values from -6 to 6
- tok_mask: int32 [32, 128], P('dp'), may hold values from 0 to 1, as said below
- tok_types: int32 [32, 128], P('dp'), may hold values from 0 to 3
- pair_mask: int32 [32, 128, 128], P('dp', 'dap'), may hold values 0 or 1
- triangle_gain: float32 [128], replicated, may hold values from 0.5 to 1.5
- triangle_input: bfloat16 [128, 512], replicated, may hold values from -0.5 to 0.5
- triangle_gating: bfloat16 [128, 128], replicated, may hold values from -0.5 to 0.5
- product_gain: float32 [128], replicated, may hold values from 0.5 to 1.5
- triangle_output: bfloat16 [128, 128], replicated, may hold values from -0.5 to 0.5
- attend_gain: float32 [128], replicated, may hold values from 0.5 to 1.5
- attend_bias: bfloat16 [128, 4], replicated, may hold values from -0.5 to 0.5
- attend_input: bfloat16 [128, 512], replicated, may hold values from -0.5 to 0.5
- attend_output: bfloat16 [128, 128], replicated, may hold values from -0.5 to 0.5
- type_table: float32 [4, 4, 4], replicated, may hold values from -4 to 4
Outputs:
- pair_out: bfloat16 [32, 128, 128, 128], P('dp', 'dap')
- pair_grad: bfloat16 [32, 128, 128, 128], P('dp', 'dap')
- grad_triangle_gain: float32 [128], replicated
- grad_triangle_input: float32 [128, 512], replicated
- grad_triangle_gating: float32 [128, 128], replicated
- grad_product_gain: float32 [128], replicated
- grad_triangle_output: float32 [128, 128], replicated
- grad_attend_gain: float32 [128], replicated
- grad_attend_bias: float32 [128, 4], replicated
- grad_attend_input: float32 [128, 512], replicated
- grad_attend_output: float32 [128, 128], replicated
- grad_type_table: float32 [4, 4, 4], replicated
Inputs may be any that keep to these rules, and one draw needn't show every extreme that they name: `tok_mask`: each crop's real tokens form a leading run of at least 64 tokens.
All inputs are finite; a program needn't handle non-finite values. No bound on the sum of `pair_mask` on one device may be relied on, other than what follows from the above.
Results may differ from a plain program's by a relative error of at most 0.035.
Values may be sent and summed in bfloat16 or wider, within the bound.
A program may use at most 128 MiB of HBM per device.

v0:
```python
from functools import partial
import jax
import jax.numpy as jnp
from jax import lax
from jax.sharding import PartitionSpec as P

EPSILON = 1e-05


def layer_norm(values, scales):
    centred = values - jnp.mean(values, axis=-1, keepdims=True)
    spread = jnp.mean(centred * centred, axis=-1, keepdims=True)
    return centred * lax.rsqrt(spread + EPSILON) * scales


def triangle_first(slab, scales, input_w, gating_w, pair_live):
    channels = slab.shape[-1]
    normed = layer_norm(slab.astype(jnp.float32), scales).astype(jnp.bfloat16)
    projected = jnp.einsum("ijc,cd->ijd", normed, input_w, preferred_element_type=jnp.float32)
    masked = pair_live[..., None]
    left_proj = (
        jax.nn.sigmoid(projected[..., channels : 2 * channels]) * projected[..., :channels] * masked
    ).astype(jnp.bfloat16)
    right_proj = (
        jax.nn.sigmoid(projected[..., 3 * channels :])
        * projected[..., 2 * channels : 3 * channels]
        * masked
    ).astype(jnp.bfloat16)
    out_gate = jax.nn.sigmoid(
        jnp.einsum("ijc,cd->ijd", normed, gating_w, preferred_element_type=jnp.float32)
    )
    return (left_proj, right_proj, out_gate)


def triangle_second(slab, product, out_gate, scales, output_w):
    normed = layer_norm(product, scales).astype(jnp.bfloat16)
    update = out_gate * jnp.einsum(
        "ijc,cd->ijd", normed, output_w, preferred_element_type=jnp.float32
    )
    return (slab.astype(jnp.float32) + update).astype(jnp.bfloat16)


def attend_first(middle, scales, bias_w):
    normed = layer_norm(middle.astype(jnp.float32), scales).astype(jnp.bfloat16)
    bias_rows = jnp.einsum(
        "rjc,ch->hrj", normed, bias_w, preferred_element_type=jnp.float32
    ).astype(jnp.bfloat16)
    return (normed, bias_rows)


def attend_second(middle, normed, bias_all, table, input_w, output_w, one_hot, key_live):
    row_count, length, channels = middle.shape
    head_count = bias_all.shape[0]
    head_size = channels // head_count
    projected = jnp.einsum("ijc,cd->ijd", normed, input_w, preferred_element_type=jnp.float32)
    query = (
        projected[..., :channels]
        .astype(jnp.bfloat16)
        .reshape(row_count, length, head_count, head_size)
    )
    keys_all = (
        projected[..., channels : 2 * channels]
        .astype(jnp.bfloat16)
        .reshape(row_count, length, head_count, head_size)
    )
    values_all = (
        projected[..., 2 * channels : 3 * channels]
        .astype(jnp.bfloat16)
        .reshape(row_count, length, head_count, head_size)
    )
    gate = jax.nn.sigmoid(projected[..., 3 * channels :])
    type_bias = jnp.einsum("ja,hab,kb->hjk", one_hot, table, one_hot)
    scores = jnp.einsum(
        "rjhd,rkhd->rhjk", query, keys_all, preferred_element_type=jnp.float32
    ) / jnp.sqrt(jnp.float32(head_size))
    scores = scores + (bias_all + type_bias)[None]
    exponent = jnp.exp(scores) * key_live[:, None, None, :]
    totals = jnp.maximum(jnp.sum(exponent, axis=-1, keepdims=True), 1.0)
    weights = (exponent / totals).astype(jnp.bfloat16)
    attended = jnp.einsum(
        "rhjk,rkhd->rjhd", weights, values_all, preferred_element_type=jnp.float32
    ).reshape(row_count, length, channels)
    gated = (gate * attended).astype(jnp.bfloat16)
    update = jnp.einsum("ijc,cd->ijd", gated, output_w, preferred_element_type=jnp.float32)
    return (middle.astype(jnp.float32) + update).astype(jnp.bfloat16)


def per_device(
    pair_rep,
    cotangent,
    tok_mask,
    tok_types,
    pair_mask,
    triangle_gain,
    triangle_input,
    triangle_gating,
    product_gain,
    triangle_output,
    attend_gain,
    attend_bias,
    attend_input,
    attend_output,
    type_table,
):
    slab = pair_rep[0]
    row_count = slab.shape[0]
    length = slab.shape[1]
    tokens = tok_mask[0].astype(jnp.float32)
    first_row = lax.axis_index("dap") * row_count
    row_tokens = lax.dynamic_slice_in_dim(tokens, first_row, row_count)
    pair_live = pair_mask[0].astype(jnp.float32) * row_tokens[:, None] * tokens[None, :]
    one_hot = (
        tok_types[0][:, None] == jnp.arange(type_table.shape[1], dtype=jnp.int32)[None, :]
    ).astype(jnp.float32)
    first_out, first_back = jax.vjp(
        partial(triangle_first, pair_live=pair_live),
        slab,
        triangle_gain,
        triangle_input,
        triangle_gating,
    )
    left_proj, right_proj, out_gate = first_out
    right_all = lax.all_gather(right_proj, "dap", axis=0, tiled=True)
    product = jnp.einsum("ikc,jkc->ijc", left_proj, right_all, preferred_element_type=jnp.float32)
    middle, second_back = jax.vjp(
        triangle_second, slab, product, out_gate, product_gain, triangle_output
    )
    third_out, third_back = jax.vjp(attend_first, middle, attend_gain, attend_bias)
    normed, bias_rows = third_out
    bias_all = lax.all_gather(bias_rows, "dap", axis=1, tiled=True).astype(jnp.float32)
    pair_out, fourth_back = jax.vjp(
        partial(attend_second, one_hot=one_hot, key_live=pair_live),
        middle,
        normed,
        bias_all,
        type_table,
        attend_input,
        attend_output,
    )
    d_middle_a, d_normed, d_bias_all, d_table, d_att_in, d_att_out = fourth_back(cotangent[0])
    d_bias_rows = lax.psum_scatter(
        d_bias_all.astype(jnp.bfloat16), "dap", scatter_dimension=1, tiled=True
    )
    d_middle_b, d_att_gain, d_att_bias = third_back((d_normed, d_bias_rows))
    attend_terms = (
        d_att_gain,
        d_att_bias.astype(jnp.float32),
        d_att_in.astype(jnp.float32),
        d_att_out.astype(jnp.float32),
        d_table,
    )
    d_middle = d_middle_a + d_middle_b
    d_slab_c, d_product, d_gate, d_prod_gain, d_tri_out = second_back(d_middle)
    d_left = jnp.einsum(
        "ijc,jkc->ikc", d_product, right_all, preferred_element_type=jnp.float32
    ).astype(jnp.bfloat16)
    d_right = lax.psum_scatter(
        jnp.einsum("ijc,ikc->jkc", d_product, left_proj, preferred_element_type=jnp.float32).astype(
            jnp.bfloat16
        ),
        "dap",
        scatter_dimension=0,
        tiled=True,
    ).astype(jnp.float32)
    d_right = d_right.astype(jnp.bfloat16)
    d_slab_d, d_tri_gain, d_tri_in, d_tri_gate = first_back((d_left, d_right, d_gate))
    d_slab = d_slab_c + d_slab_d
    triangle_terms = (
        d_tri_gain,
        d_tri_in.astype(jnp.float32),
        d_tri_gate.astype(jnp.float32),
        d_prod_gain,
        d_tri_out.astype(jnp.float32),
    )
    summed_all = lax.psum(triangle_terms + attend_terms, ("dap", "dp"))
    triangle_summed = summed_all[:5]
    attend_summed = summed_all[5:]
    factor = (length * length * lax.axis_size("dp")) ** (-0.5)
    return (
        pair_out[None],
        d_slab[None],
        triangle_summed[0] * factor,
        triangle_summed[1] * factor,
        triangle_summed[2] * factor,
        triangle_summed[3] * factor,
        triangle_summed[4] * factor,
        attend_summed[0] * factor,
        attend_summed[1] * factor,
        attend_summed[2] * factor,
        attend_summed[3] * factor,
        attend_summed[4] * factor,
    )


def solution(mesh):
    return jax.shard_map(
        per_device,
        mesh=mesh,
        in_specs=(
            P("dp", "dap", None, None),
            P("dp", "dap", None, None),
            P("dp", None),
            P("dp", None),
            P("dp", "dap", None),
            P(),
            P(),
            P(),
            P(),
            P(),
            P(),
            P(),
            P(),
            P(),
            P(),
        ),
        out_specs=(
            P("dp", "dap", None, None),
            P("dp", "dap", None, None),
            P(),
            P(),
            P(),
            P(),
            P(),
            P(),
            P(),
            P(),
            P(),
            P(),
        ),
        check_vma=False,
    )
```

profile of v0, /device:TPU:1, one launch (start us, length us, event | category | flops | bytes accessed | tf_op | source)
XLA Modules:
  0.0 484.0 jit_solution(14713057218166650713)
XLA Ops:
  11.1 2.7 multiply_convert_fusion.1
  18.8 47.5 %all-gather.2.cloned.1.call-done = bf16[128,128,128]{2,1,0:T(8,128)(2,1)} async-done(((bf16[32,128,128]{2,1,0:T(8,128)(2,1)}), bf16[128,128,128]{2,1,0:T(8,128)(2,1)}) %all-gather.2.cloned.1.call-update) | async-done | bytes 4194320 | tf_op jit(solution)/shard_map/all_gather | solution.py:123
  66.3 6.7 %copy.133 = bf16[128,128,128]{1,0,2:T(8,128)(2,1)} copy(bf16[128,128,128]{2,1,0:T(8,128)(2,1)} %all-gather.2.cloned.1.call-done) | data formatting | bytes 8388608 | tf_op jit(solution)/shard_map/all_gather | solution.py:123
  73.1 4.8 bitcast_reduce_fusion
  79.7 2.5 convert_reduce_fusion
  82.6 3.3 fusion.166
  87.6 2.9 copy.206
  90.5 3.7 fusion.164
  94.2 2.3 copy.139
  98.1 5.6 %all_gather.7 = bf16[4,128,128]{2,0,1:T(4,128)(2,1)S(1)} all-gather(bf16[4,32,128]{2,0,1:T(4,128)(2,1)S(1)} %fusion.93), channel_id=1, replica_groups=mesh['dap'=4,'dp'=32] {'dap'}, dimensions={1}, use_global_device_ids=true | all-gather | bytes 163840 | tf_op jit(solution)/shard_map/all_gather | solution.py:130
  105.8 2.4 copy.140
  108.2 2.3 copy.141
  110.4 4.3 multiply_reduce_fusion
  116.4 4.5 fusion.4
  121.0 5.5 %fusion.161 = (bf16[4,128,128]{1,2,0:T(8,128)(2,1)S(1)}, f32[32,4,128,128]{2,3,1,0:T(8,128)S(1)}, bf16[32,4,128,128]{2,3,1,0:T(8,128)(2,1)S(1)}) fusion(f32[4,128,128]{1,2,0:T(8,128)} %copy-done.27, f32[32,4,128,128]{2,3,1,0:T(8,128)S(1)} %get-tuple-element.96, f32[32,128]{1,0:T(8,128)S(1)} %copy-done.44, f32[32,4,128]{2,1,0:T(4,128)S(1)} %get-tuple-element.84, ...), kind=kLoop, calls=%fused_computation.231 | loop fusion | flops 23003136 | bytes 25706496 | tf_op jit(solution)/shard_map/transpose(jvp())/reduce_sum | solution.py:76
  126.5 3.5 fusion.70
  130.0 3.3 fusion.67
  133.4 2.5 fusion.167
  135.9 3.3 fusion.168
  140.2 4.6 fusion.41
  148.0 28.9 %all-reduce.14.cloned.1.call-done = bf16[4,128,128]{2,0,1:T(4,128)(2,1)} async-done(((bf16[4,128,128]{2,0,1:T(4,128)(2,1)}), bf16[4,128,128]{2,0,1:T(4,128)(2,1)}) %all-reduce.14.cloned.1.call-update) | async-done | bytes 131088
  176.9 2.5 fusion.47
  188.2 3.3 fusion.63
  191.5 6.8 %copy.160 = bf16[128,128,128]{1,0,2:T(8,128)(2,1)} copy(bf16[128,128,128]{2,1,0:T(8,128)(2,1)} %fusion.63) | data formatting | bytes 8388608 | tf_op jit(solution)/shard_map/ijc,ikc->jkc/dot_general | solution.py:158
  201.3 2.3 copy.172
  203.8 2.4 fusion.90
  206.3 3.9 fusion.85
  217.5 27.1 %reduce-scatter.2.cloned.1.call-done = bf16[32,128,128]{1,2,0:T(8,128)(2,1)} async-done(((bf16[128,128,128]{1,2,0:T(8,128)(2,1)}), bf16[32,128,128]{1,2,0:T(8,128)(2,1)}) %reduce-scatter.2.cloned.1.call-update) | async-done | bytes 1048592 | tf_op jit(solution)/shard_map/reduce_scatter | solution.py:157
  244.7 5.1 %fusion.60 = (f32[32,128,128]{1,2,0:T(8,128)S(1)}, f32[32,128,128]{1,2,0:T(8,128)S(1)}, f32[32,128,128]{1,2,0:T(8,128)S(1)}, f32[32,128,128]{1,2,0:T(8,128)S(1)}) fusion(bf16[32,128,128]{1,2,0:T(8,128)(2,1)} %reduce-scatter.2.cloned.1.call-done, f32[32,128]{1,0:T(8,128)S(1)} %copy-done.45, f32[32,128,512]{1,2,0:T(8,128)} %copy-done.2, ...), kind=kLoop, calls=%fused_computation.101 | loop fusion | flops 10485760 | bytes 18890752 | tf_op jit(solution)/shard_map/transpose(jvp())/mul | solution.py:25
  253.0 3.3 fusion.39
  260.2 65.8 %all-reduce.9 = (f32[128]{0:T(128)S(1)}, f32[128]{0:T(128)S(1)}, f32[128]{0:T(128)S(1)}, f32[128,4]{0,1:T(4,128)S(1)}, f32[4,4,4]{1,2,0:T(4,128)S(1)}) all-reduce(f32[128]{0:T(128)S(1)} %get-tuple-element.52, f32[128]{0:T(128)S(1)} %get-tuple-element.48, f32[128]{0:T(128)S(1)} %copy-done.70, ...), channel_id=1, replica_groups=mesh['dap'=4,'dp'=32] {'dap','dp'}, use_global_device_ids=true, to_apply=%region_18.0 | all-reduce | flops 960 | bytes 7680 | tf_op jit(solution)/shard_map/psum | solution.py:175
  328.4 144.0 %all-reduce.16.cloned.1.call-done = (f32[128,512]{1,0:T(8,128)}, f32[128,128]{1,0:T(8,128)}, f32[128,128]{1,0:T(8,128)}, f32[128,512]{1,0:T(8,128)}, f32[128,128]{1,0:T(8,128)}) async-done(((f32[128,512]{1,0:T(8,128)}, f32[128,128]{1,0:T(8,128)}, f32[128,128]{1,0:T(8,128)}, f32[128,512]{1,0:T(8,128)}, f32[128,128]{1,0:T(8,128)}), (f32[128,512]{1,0:T(8,128)}, f32[128,128]{1,0:T(8,128)}, ...) | async-done | bytes 720912 | tf_op jit(solution)/shard_map/psum | solution.py:175
  (219 shorter events, 55.1 us)
Async XLA Ops:
  7.2 75.4 %copy-start = (bf16[128,512]{1,0:T(8,128)(2,1)S(1)}, bf16[128,512]{1,0:T(8,128)(2,1)}, u32[]{:S(2)}) copy-start(bf16[128,512]{1,0:T(8,128)(2,1)} %param.27) | copy-start | bytes 393220
  7.2 59.1 %all-gather.2.cloned.1.call-start = ((), (), s32[]{:S(2)}) async-start(), calls=%async_computation.1 | async-start | bytes 5242880 | tf_op jit(solution)/shard_map/all_gather | solution.py:123
  9.6 69.8 %copy-start.33 = (f32[32,128]{1,0:T(8,128)}, f32[32,128]{1,0:T(8,128)S(1)}, u32[]{:S(2)}) copy-start(f32[32,128]{1,0:T(8,128)S(1)} %fusion.126) | copy-start | bytes 49156
  11.0 3.6 copy-start.2
  11.1 3.5 copy-start.43
  16.0 160.9 %all-reduce.14.cloned.1.call-start = ((), (), s32[]{:S(2)}) async-start(), calls=%async_computation.3 | async-start | bytes 262144
  82.2 3.8 copy-start.8
  82.2 14.2 %copy-start.35 = (f32[32,128]{1,0:T(8,128)}, f32[32,128]{1,0:T(8,128)S(1)}, u32[]{:S(2)}) copy-start(f32[32,128]{1,0:T(8,128)S(1)} %broadcast_multiply_fusion.5) | copy-start | bytes 49156
  82.6 3.4 copy-start.50
  82.6 13.8 %copy-start.39 = (f32[32,128]{1,0:T(8,128)}, f32[32,128]{1,0:T(8,128)S(1)}, u32[]{:S(2)}) copy-start(f32[32,128]{1,0:T(8,128)S(1)} %fusion.128) | copy-start | bytes 49156
  105.8 10.6 %copy-start.27 = (f32[4,128,128]{1,2,0:T(8,128)}, f32[4,128,128]{1,2,0:T(8,128)S(1)}, u32[]{:S(2)}) copy-start(f32[4,128,128]{1,2,0:T(8,128)S(1)} %copy.145) | copy-start | bytes 786436
  110.4 4.3 copy-start.19
  110.4 4.3 copy-start.24
  110.4 4.3 copy-start.56
  116.4 4.6 copy-start.31
  126.5 3.5 copy-start.22
  140.0 104.7 %reduce-scatter.2.cloned.1.call-start = ((), (), s32[]{:S(2)}) async-start(), calls=%async_computation.2 | async-start | bytes 5242880 | tf_op jit(solution)/shard_map/reduce_scatter | solution.py:157
  140.2 6.0 %copy-start.28 = (bf16[32,4,128,32]{2,3,1,0:T(8,128)(2,1)S(1)}, bf16[32,4,128,32]{2,3,1,0:T(8,128)(2,1)}, u32[]{:S(2)}) copy-start(bf16[32,4,128,32]{2,3,1,0:T(8,128)(2,1)} %fusion.70) | copy-start | bytes 3145732
  140.2 6.0 %copy-start.29 = (bf16[32,4,128,32]{2,3,1,0:T(8,128)(2,1)S(1)}, bf16[32,4,128,32]{2,3,1,0:T(8,128)(2,1)}, u32[]{:S(2)}) copy-start(bf16[32,4,128,32]{2,3,1,0:T(8,128)(2,1)} %fusion.67) | copy-start | bytes 3145732
  140.2 6.0 %copy-start.30 = (bf16[32,4,32,128]{3,2,1,0:T(8,128)(2,1)S(1)}, bf16[32,4,32,128]{3,2,1,0:T(8,128)(2,1)}, u32[]{:S(2)}) copy-start(bf16[32,4,32,128]{3,2,1,0:T(8,128)(2,1)} %fusion.168) | copy-start | bytes 3145732
  146.2 30.7 %copy-start.36 = (f32[32,128]{1,0:T(8,128)S(1)}, f32[32,128]{1,0:T(8,128)}, u32[]{:S(2)}) copy-start(f32[32,128]{1,0:T(8,128)} %copy-done.35) | copy-start | bytes 49156
  146.2 30.7 %copy-start.69 = (f32[128]{0:T(128)S(1)}, f32[128]{0:T(128)}, u32[]{:S(2)}) copy-start(f32[128]{0:T(128)} %param.25) | copy-start | bytes 1540
  146.2 30.7 %copy-start.72 = (bf16[128,4]{0,1:T(4,128)(2,1)S(1)}, bf16[128,4]{0,1:T(4,128)(2,1)}, u32[]{:S(2)}) copy-start(bf16[128,4]{0,1:T(4,128)(2,1)} %param.26) | copy-start | bytes 3076
  148.0 31.4 %copy-start.51 = (f32[32,128]{1,0:T(8,128)S(1)}, f32[32,128]{1,0:T(8,128)}, u32[]{:S(2)}) copy-start(f32[32,128]{1,0:T(8,128)} %copy-done.50) | copy-start | bytes 49156
  148.0 31.5 %copy-start.40 = (f32[32,128]{1,0:T(8,128)S(1)}, f32[32,128]{1,0:T(8,128)}, u32[]{:S(2)}) copy-start(f32[32,128]{1,0:T(8,128)} %copy-done.39) | copy-start | bytes 49156
  176.9 4.6 copy-start.20
  198.3 274.0 %all-reduce.16.cloned.1.call-start = ((), (), s32[]{:S(2)}) async-start(), calls=%async_computation.4 | async-start | bytes 1441792 | tf_op jit(solution)/shard_map/psum | solution.py:175
  199.9 3.7 copy-start.64
  206.3 5.3 %copy-start.7 = (f32[32,128,128]{1,2,0:T(8,128)S(1)}, f32[32,128,128]{1,2,0:T(8,128)}, u32[]{:S(2)}) copy-start(f32[32,128,128]{1,2,0:T(8,128)} %get-tuple-element.90) | copy-start | bytes 6291460
  216.3 28.3 %copy-start.45 = (f32[32,128]{1,0:T(8,128)S(1)}, f32[32,128]{1,0:T(8,128)}, u32[]{:S(2)}) copy-start(f32[32,128]{1,0:T(8,128)} %copy-done.43) | copy-start | bytes 49156
  217.5 32.2 %copy-start.53 = (bf16[128,512]{1,0:T(8,128)(2,1)S(1)}, bf16[128,512]{1,0:T(8,128)(2,1)}, u32[]{:S(2)}) copy-start(bf16[128,512]{1,0:T(8,128)(2,1)} %param.21) | copy-start | bytes 393220
  257.8 219.4 %copy-start.1 = (bf16[128,512]{1,0:T(8,128)(2,1)S(1)}, bf16[128,512]{1,0:T(8,128)(2,1)}, u32[]{:S(2)}) copy-start(bf16[128,512]{1,0:T(8,128)(2,1)} %param.27) | copy-start | bytes 393220
  (47 other events, 82.1 us)
Sparse Core Ops, SparseCore 0:
  16.1 50.2 all-gather.1
  140.1 36.7 all-reduce.13
  198.5 46.1 reduce-scatter.1
  327.4 144.9 all-reduce.15
where the time goes:
time: 494 us; the launch traced here: 484 us
  waiting for transfers between devices  248 us (50%)
  blocking collectives  71.4 us (14%)
  matrix products  66.2 us (13%)
  local copies, waits for them, and re-layouts  48.2 us (10%)
  other arithmetic  34.7 us (7%)
  between operations  15.4 us (3%)
    psum x1, waiting for transfers between devices, per_device(): summed_all = lax.psum(triangle_terms + attend_terms, ('dap', 'dp'))  144 us
    psum x1, blocking collectives, per_device(): summed_all = lax.psum(triangle_terms + attend_terms, ('dap', 'dp'))  65.8 us
    all_gather x1, waiting for transfers between devices, per_device(): right_all = lax.all_gather(right_proj, 'dap', axis=0, tiled=True)  47.5 us
    unnamed x5, waiting for transfers between devices  29 us
    reduce_scatter x1, waiting for transfers between devices, per_device(): lax.psum_scatter(jnp.einsum('ijc,ikc->jkc', d_product, left_proj, preferr...  27.1 us
    unnamed x158, local copies, waits for them, and re-layouts  19.2 us
    dot_general x3, matrix products, attend_second(): jnp.einsum('rjhd,rkhd->rhjk', query, keys_all, preferred_element_type=jnp...  11.1 us
    dot_general x3, matrix products, attend_second(): jnp.einsum('rhjk,rkhd->rjhd', weights, values_all, preferred_element_type...  10.3 us
  transfers between devices with their start and end apart: 4, of which 4 were waited for; matrix products, arithmetic and copies ran while one was open for 5% of the time, Pallas kernels for 0%

commit v1 on v0

--- a/solution.py
+++ b/solution.py
@@ -1,3 +1,4 @@
+import functools
 from functools import partial
 import jax
 import jax.numpy as jnp
@@ -5,6 +6,14 @@
 from jax.sharding import PartitionSpec as P
 
 EPSILON = 1e-05
+
+
+def try_all_tiles_up(target, net_axis, mesh_ax):
+    moved = lax.psum(lax.psum(target, net_axis), mesh_ax)
+    return moved
+
+
+_do_packet = functools.partial(try_all_tiles_up, net_axis="dp", mesh_ax="dap")
 
 
 def layer_norm(values, scales):
@@ -172,7 +181,7 @@
         d_prod_gain,
         d_tri_out.astype(jnp.float32),
     )
-    summed_all = lax.psum(triangle_terms + attend_terms, ("dap", "dp"))
+    summed_all = _do_packet(triangle_terms + attend_terms)
     triangle_summed = summed_all[:5]
     attend_summed = summed_all[5:]
     factor = (length * length * lax.axis_size("dp")) ** (-0.5)

time: 494 us -> 670 us (1.36)
  blocking collectives: 71.4 us -> 197 us
  waiting for transfers between devices: 248 us -> 295 us
    psum x1 -> x2, blocking collectives: 65.8 us -> 192 us  [try_all_tiles_up(): moved = lax.psum(lax.psum(target, net_axis), mesh_ax)]
    psum x1 -> x2, waiting for transfers between devices: 144 us -> 192 us  [try_all_tiles_up(): moved = lax.psum(lax.psum(target, net_axis), mesh_ax)]
    unnamed x158 -> x156, local copies, waits for them, and re-layouts: 19.2 us -> 20.2 us
    unnamed x5 -> x6, waiting for transfers between devices: 29 us -> 29 us
  transfers between devices with their start and end apart: 4 -> 5, of which waited for: 4 -> 5; matrix products, arithmetic and copies ran while one was open for 5% -> 5% of each run, Pallas kernels for 0% -> 0%
where the time goes in v1:
time: 670 us; the launch traced here: 660 us
  waiting for transfers between devices  295 us (44%)
  blocking collectives  197 us (29%)
  matrix products  67.2 us (10%)
  local copies, waits for them, and re-layouts  49.1 us (7%)
  other arithmetic  35.2 us (5%)
  between operations  15.4 us (2%)
    psum x2, blocking collectives, try_all_tiles_up(): moved = lax.psum(lax.psum(target, net_axis), mesh_ax)  192 us
    psum x2, waiting for transfers between devices, try_all_tiles_up(): moved = lax.psum(lax.psum(target, net_axis), mesh_ax)  192 us
    all_gather x1, waiting for transfers between devices, per_device(): right_all = lax.all_gather(right_proj, 'dap', axis=0, tiled=True)  47.5 us
    unnamed x6, waiting for transfers between devices  29 us
    reduce_scatter x1, waiting for transfers between devices, per_device(): lax.psum_scatter(jnp.einsum('ijc,ikc->jkc', d_product, left_proj, preferr...  27.2 us
    unnamed x156, local copies, waits for them, and re-layouts  20.2 us
  transfers between devices with their start and end apart: 5, of which 5 were waited for; matrix products, arithmetic and copies ran while one was open for 5% of the time, Pallas kernels for 0%

profile of v1, /device:TPU:1, one launch (start us, length us, event | category | flops | bytes accessed | tf_op | source)
XLA Modules:
  0.0 660.1 jit_solution(11335494049353224839)
XLA Ops:
  11.1 2.7 multiply_convert_fusion.1
  18.8 47.5 %all-gather.2.cloned.1.call-done = bf16[128,128,128]{2,1,0:T(8,128)(2,1)} async-done(((bf16[32,128,128]{2,1,0:T(8,128)(2,1)}), bf16[128,128,128]{2,1,0:T(8,128)(2,1)}) %all-gather.2.cloned.1.call-update) | async-done | bytes 4194320 | tf_op jit(solution)/shard_map/all_gather | solution.py:132
  66.4 6.7 %copy.133 = bf16[128,128,128]{1,0,2:T(8,128)(2,1)} copy(bf16[128,128,128]{2,1,0:T(8,128)(2,1)} %all-gather.2.cloned.1.call-done) | data formatting | bytes 8388608 | tf_op jit(solution)/shard_map/all_gather | solution.py:132
  73.1 4.8 bitcast_reduce_fusion
  79.7 2.5 convert_reduce_fusion
  82.7 3.3 fusion.166
  87.7 2.9 copy.206
  90.6 3.7 fusion.164
  98.2 5.6 all_gather.7
  105.8 2.4 copy.140
  110.5 4.3 multiply_reduce_fusion
  116.5 4.5 fusion.4
  121.1 5.5 fusion.161
  126.6 3.5 fusion.70
  130.1 3.3 fusion.67
  133.4 2.5 fusion.167
  136.0 3.3 fusion.168
  140.3 4.6 fusion.41
  148.0 28.9 %all-reduce.17.cloned.1.call-done = bf16[4,128,128]{2,0,1:T(4,128)(2,1)} async-done(((bf16[4,128,128]{2,0,1:T(4,128)(2,1)}), bf16[4,128,128]{2,0,1:T(4,128)(2,1)}) %all-reduce.17.cloned.1.call-update) | async-done | bytes 131088
  177.0 2.5 fusion.47
  187.8 3.3 fusion.63
  191.1 6.7 %copy.160 = bf16[128,128,128]{1,0,2:T(8,128)(2,1)} copy(bf16[128,128,128]{2,1,0:T(8,128)(2,1)} %fusion.63) | data formatting | bytes 8388608 | tf_op jit(solution)/shard_map/ijc,ikc->jkc/dot_general | solution.py:167
  203.3 2.4 fusion.90
  205.8 3.9 fusion.85
  217.0 27.2 %reduce-scatter.2.cloned.1.call-done = bf16[32,128,128]{1,2,0:T(8,128)(2,1)} async-done(((bf16[128,128,128]{1,2,0:T(8,128)(2,1)}), bf16[32,128,128]{1,2,0:T(8,128)(2,1)}) %reduce-scatter.2.cloned.1.call-update) | async-done | bytes 1048592 | tf_op jit(solution)/shard_map/reduce_scatter | solution.py:166
  244.2 5.1 fusion.60
  253.3 3.5 fusion.39
  258.4 157.6 %all-reduce.9 = (f32[128]{0:T(128)S(1)}, f32[128]{0:T(128)S(1)}, f32[128]{0:T(128)S(1)}, f32[128,4]{0,1:T(4,128)S(1)}, f32[4,4,4]{1,2,0:T(4,128)S(1)}) all-reduce(f32[128]{0:T(128)S(1)} %get-tuple-element.52, f32[128]{0:T(128)S(1)} %get-tuple-element.48, f32[128]{0:T(128)S(1)} %get-tuple-element.50, ...), channel_id=1, replica_groups=mesh['dap'=4,'dp'=32] {'dp'}, use_global_device_ids=true, to_apply=%region_18.0 | all-reduce | flops 960 | bytes 7680 | tf_op jit(solution)/shard_map/psum | solution.py:12
  416.0 34.2 %all-reduce.11 = (f32[128]{0:T(128)S(1)}, f32[128]{0:T(128)S(1)}, f32[128]{0:T(128)S(1)}, f32[128,4]{0,1:T(4,128)S(1)}, f32[4,4,4]{1,2,0:T(4,128)S(1)}) all-reduce(f32[128]{0:T(128)S(1)} %get-tuple-element.54, f32[128]{0:T(128)S(1)} %get-tuple-element.55, f32[128]{0:T(128)S(1)} %get-tuple-element.56, ...), channel_id=1, replica_groups=mesh['dap'=4,'dp'=32] {'dap'}, use_global_device_ids=true, to_apply=%region_19.0 | all-reduce | flops 960 | bytes 7680 | tf_op jit(solution)/shard_map/psum | solution.py:12
  452.2 132.2 %all-reduce.19.cloned.1.call-done = (f32[128,512]{1,0:T(8,128)}, f32[128,128]{1,0:T(8,128)}, f32[128,128]{1,0:T(8,128)}, f32[128,512]{1,0:T(8,128)}, f32[128,128]{1,0:T(8,128)}) async-done(((f32[128,512]{1,0:T(8,128)}, f32[128,128]{1,0:T(8,128)}, f32[128,128]{1,0:T(8,128)}, f32[128,512]{1,0:T(8,128)}, f32[128,128]{1,0:T(8,128)}), (f32[128,512]{1,0:T(8,128)}, f32[128,128]{1,0:T(8,128)}, ...) | async-done | bytes 720912 | tf_op jit(solution)/shard_map/psum | solution.py:12
  584.5 2.3 copy.173
  589.1 59.4 %all-reduce.21.cloned.1.call-done = (f32[128,512]{1,0:T(8,128)}, f32[128,128]{1,0:T(8,128)}, f32[128,128]{1,0:T(8,128)}, f32[128,512]{1,0:T(8,128)}, f32[128,128]{1,0:T(8,128)}) async-done(((f32[128,512]{1,0:T(8,128)}, f32[128,128]{1,0:T(8,128)}, f32[128,128]{1,0:T(8,128)}, f32[128,512]{1,0:T(8,128)}, f32[128,128]{1,0:T(8,128)}), (f32[128,512]{1,0:T(8,128)}, f32[128,128]{1,0:T(8,128)}, ...) | async-done | bytes 720912 | tf_op jit(solution)/shard_map/psum | solution.py:12
  (221 shorter events, 61.8 us)
Async XLA Ops:
  7.2 75.5 %copy-start = (bf16[128,512]{1,0:T(8,128)(2,1)S(1)}, bf16[128,512]{1,0:T(8,128)(2,1)}, u32[]{:S(2)}) copy-start(bf16[128,512]{1,0:T(8,128)(2,1)} %param.27) | copy-start | bytes 393220
  7.2 59.2 %all-gather.2.cloned.1.call-start = ((), (), s32[]{:S(2)}) async-start(), calls=%async_computation.1 | async-start | bytes 5242880 | tf_op jit(solution)/shard_map/all_gather | solution.py:132
  9.6 69.9 %copy-start.33 = (f32[32,128]{1,0:T(8,128)}, f32[32,128]{1,0:T(8,128)S(1)}, u32[]{:S(2)}) copy-start(f32[32,128]{1,0:T(8,128)S(1)} %fusion.126) | copy-start | bytes 49156
  11.0 3.6 copy-start.2
  16.0 161.0 %all-reduce.17.cloned.1.call-start = ((), (), s32[]{:S(2)}) async-start(), calls=%async_computation.3 | async-start | bytes 262144
  82.3 3.8 copy-start.8
  82.3 14.2 %copy-start.35 = (f32[32,128]{1,0:T(8,128)}, f32[32,128]{1,0:T(8,128)S(1)}, u32[]{:S(2)}) copy-start(f32[32,128]{1,0:T(8,128)S(1)} %broadcast_multiply_fusion.5) | copy-start | bytes 49156
  82.7 13.8 %copy-start.39 = (f32[32,128]{1,0:T(8,128)}, f32[32,128]{1,0:T(8,128)S(1)}, u32[]{:S(2)}) copy-start(f32[32,128]{1,0:T(8,128)S(1)} %fusion.128) | copy-start | bytes 49156
  105.8 10.7 %copy-start.27 = (f32[4,128,128]{1,2,0:T(8,128)}, f32[4,128,128]{1,2,0:T(8,128)S(1)}, u32[]{:S(2)}) copy-start(f32[4,128,128]{1,2,0:T(8,128)S(1)} %copy.145) | copy-start | bytes 786436
  110.5 4.3 copy-start.19
  110.5 4.3 copy-start.24
  110.5 4.3 copy-start.56
  116.5 4.5 copy-start.31
  126.6 3.5 copy-start.22
  140.0 104.1 %reduce-scatter.2.cloned.1.call-start = ((), (), s32[]{:S(2)}) async-start(), calls=%async_computation.2 | async-start | bytes 5242880 | tf_op jit(solution)/shard_map/reduce_scatter | solution.py:166
  140.3 6.0 copy-start.28
  140.3 6.0 copy-start.29
  140.3 6.0 copy-start.30
  146.3 30.7 %copy-start.36 = (f32[32,128]{1,0:T(8,128)S(1)}, f32[32,128]{1,0:T(8,128)}, u32[]{:S(2)}) copy-start(f32[32,128]{1,0:T(8,128)} %copy-done.35) | copy-start | bytes 49156
  146.3 30.7 %copy-start.69 = (f32[128]{0:T(128)S(1)}, f32[128]{0:T(128)}, u32[]{:S(2)}) copy-start(f32[128]{0:T(128)} %param.25) | copy-start | bytes 1540
  146.3 30.7 %copy-start.71 = (bf16[128,4]{0,1:T(4,128)(2,1)S(1)}, bf16[128,4]{0,1:T(4,128)(2,1)}, u32[]{:S(2)}) copy-start(bf16[128,4]{0,1:T(4,128)(2,1)} %param.26) | copy-start | bytes 3076
  148.0 31.5 %copy-start.51 = (f32[32,128]{1,0:T(8,128)S(1)}, f32[32,128]{1,0:T(8,128)}, u32[]{:S(2)}) copy-start(f32[32,128]{1,0:T(8,128)} %copy-done.50) | copy-start | bytes 49156
  148.0 31.5 %copy-start.40 = (f32[32,128]{1,0:T(8,128)S(1)}, f32[32,128]{1,0:T(8,128)}, u32[]{:S(2)}) copy-start(f32[32,128]{1,0:T(8,128)} %copy-done.39) | copy-start | bytes 49156
  177.0 4.1 copy-start.20
  197.8 386.6 %all-reduce.19.cloned.1.call-start = ((), (), s32[]{:S(2)}) async-start(), calls=%async_computation.4 | async-start | bytes 1441792 | tf_op jit(solution)/shard_map/psum | solution.py:12
  199.4 3.7 copy-start.64
  205.8 5.3 copy-start.7
  215.8 28.4 %copy-start.45 = (f32[32,128]{1,0:T(8,128)S(1)}, f32[32,128]{1,0:T(8,128)}, u32[]{:S(2)}) copy-start(f32[32,128]{1,0:T(8,128)} %copy-done.43) | copy-start | bytes 49156
  217.0 32.3 %copy-start.53 = (bf16[128,512]{1,0:T(8,128)(2,1)S(1)}, bf16[128,512]{1,0:T(8,128)(2,1)}, u32[]{:S(2)}) copy-start(bf16[128,512]{1,0:T(8,128)(2,1)} %param.21) | copy-start | bytes 393220
  253.3 3.6 copy-start.47
  256.9 391.6 %all-reduce.21.cloned.1.call-start = ((), (), s32[]{:S(2)}) async-start(), calls=%async_computation.5 | async-start | bytes 1441792 | tf_op jit(solution)/shard_map/psum | solution.py:12
  584.4 68.9 %copy-start.1 = (bf16[128,512]{1,0:T(8,128)(2,1)S(1)}, bf16[128,512]{1,0:T(8,128)(2,1)}, u32[]{:S(2)}) copy-start(bf16[128,512]{1,0:T(8,128)(2,1)} %param.27) | copy-start | bytes 393220
  (47 other events, 84.3 us)
Sparse Core Ops, SparseCore 0:
  16.1 50.2 all-gather.1
  140.2 36.7 all-reduce.16
  198.0 46.1 reduce-scatter.1
  257.0 327.3 all-reduce.18
  587.4 61.0 all-reduce.20
